TPU v7x, 256 devices: a whole 4x4x8 slice. The times are simulated.
256 devices in a mesh: enc: 16 (over z, core), vocab: 8 (over x, y_hi), grp: 2 (over y_lo).
Axes of the slice: x: 4, y: 4 (y_hi: 2, y_lo: 2; y = y_hi * 2 + y_lo), z: 8, core: 2. Of those that a mesh axis runs over, the one named last changes fastest.
Arguments:
- hidden: bfloat16 [12288, 1024], P('enc', ('vocab', 'grp')), may hold values from -6 to 6
- dense_weight: bfloat16 [1024, 1024], P('enc'), may hold values from -0.1875 to 0.1875
- head_weight: bfloat16 [1024, 126976], P('enc', ('vocab', 'grp')), may hold values from -0.1875 to 0.1875
- head_bias: float32 [126976], P(('vocab', 'grp')), may hold values from -4 to 4
- lengths: int32 [48], P('enc'), may hold values from 64 to 256, as said below
- queries: bfloat16 [128, 126976], P('enc', ('vocab', 'grp')), may hold values from -0.25 to 0.25283518
- positives: int32 [128], replicated, may hold values from 0 to 47
Outputs:
- batch_loss: float32 [], replicated
- query_grad: float32 [128, 126976], P('enc', ('vocab', 'grp'))
- passage_grad: float32 [48, 126976], P('enc', ('vocab', 'grp'))
Inputs may be any that keep to these rules, and one draw needn't show every extreme that they name: `lengths`: each 3 passages in a row hold, among their first two, one with 256 valid tokens and one with 64.
All inputs are finite; a program needn't handle non-finite values.
Results may differ from a plain program's by a relative error of at most 0.035.
Values may be sent and summed in bfloat16 or wider, within the bound.
A program may use at most 128 MiB of HBM per device.

v0:
```python
import jax
import jax.numpy as jnp
from jax import lax
from jax.sharding import PartitionSpec as P


def finish_norm(pre_act):
    activated = jax.nn.gelu(pre_act, approximate=False)
    center = jnp.mean(activated, axis=-1, keepdims=True)
    spread = jnp.mean(jnp.square(activated - center), axis=-1, keepdims=True)
    return ((activated - center) * lax.rsqrt(spread + 1e-05)).astype(jnp.bfloat16)


def project(in_rows, dense_weight):
    pre_act = jnp.dot(
        in_rows,
        lax.all_gather(dense_weight, "enc", axis=0, tiled=True),
        preferred_element_type=jnp.float32,
    )
    return finish_norm(pre_act)


def pool_reps(logits, token_counts, seq_len):
    passages = token_counts.shape[0]
    by_passage = logits.reshape(passages, seq_len, logits.shape[1])
    positions = lax.broadcasted_iota(jnp.int32, (passages, seq_len), 1)
    is_valid = positions < token_counts[:, None]
    masked = jnp.where(is_valid[:, :, None], by_passage, -jnp.inf)
    peak_val = jnp.max(masked, axis=1)
    return jnp.log1p(jnp.maximum(peak_val, 0.0)).astype(jnp.bfloat16)


def softmax_grads(scores, chosen):
    peak_val = jnp.max(scores, axis=1, keepdims=True)
    log_total = jnp.log(jnp.sum(jnp.exp(scores - peak_val), axis=1, keepdims=True)) + peak_val
    columns = lax.broadcasted_iota(jnp.int32, scores.shape, 1)
    is_positive = columns == chosen[:, None]
    picked_score = jnp.sum(jnp.where(is_positive, scores, 0.0), axis=1)
    batch_loss = jnp.sum(log_total[:, 0] - picked_score)
    score_grad = (jnp.exp(scores - log_total) - is_positive.astype(jnp.float32)).astype(
        jnp.bfloat16
    )
    return (batch_loss, score_grad)


def per_device(hidden, dense_weight, head_weight, head_bias, lengths, queries, positives):
    pass_dev = lengths.shape[0]
    seq_len = hidden.shape[0] // pass_dev
    enc_index = lax.axis_index("enc")
    features_all = lax.all_gather(hidden, ("vocab", "grp"), axis=1, tiled=True)
    normed = project(features_all, dense_weight)
    logits = jnp.dot(
        normed,
        lax.all_gather(head_weight, "enc", axis=0, tiled=True),
        preferred_element_type=jnp.float32,
    )
    pass_reps = pool_reps(logits + head_bias, lengths, seq_len)
    all_queries = lax.all_gather(queries, "enc", axis=0, tiled=True)
    partial_value = lax.dot_general(
        all_queries, pass_reps, (((1,), (1,)), ((), ())), preferred_element_type=jnp.float32
    )
    local_scores = lax.psum(partial_value, ("vocab", "grp"))
    scores = lax.all_gather(local_scores, "enc", axis=1, tiled=True)
    loss_sum, score_grad = softmax_grads(scores, positives)
    batch_loss = loss_sum / scores.shape[0]
    own_grad = lax.dynamic_slice_in_dim(score_grad, enc_index * pass_dev, pass_dev, 1)
    query_grad = lax.psum_scatter(
        jnp.dot(own_grad, pass_reps, preferred_element_type=jnp.float32),
        "enc",
        scatter_dimension=0,
        tiled=True,
    )
    passage_grad = lax.dot_general(
        own_grad, all_queries, (((0,), (0,)), ((), ())), preferred_element_type=jnp.float32
    )
    return (batch_loss, query_grad, passage_grad)


def solution(mesh):
    placed = (
        P("enc", ("vocab", "grp")),
        P("enc", None),
        P("enc", ("vocab", "grp")),
        P(("vocab", "grp")),
        P("enc"),
        P("enc", ("vocab", "grp")),
        P(),
    )
    return jax.shard_map(
        per_device,
        mesh=mesh,
        in_specs=placed,
        out_specs=(P(), P("enc", ("vocab", "grp")), P("enc", ("vocab", "grp"))),
        check_vma=False,
    )
```

profile of v0, /device:TPU:2, one launch (start us, length us, event | category | flops | bytes accessed | tf_op | source)
XLA Modules:
  0.0 363.2 jit_solution(3995243074012879067)
XLA Ops:
  7.2 0.0 all-gather.6.cloned.1.call-start
  7.2 0.7 all-gather.6.cloned.1.call-update
  7.9 0.0 all-gather.8.cloned.1.call-start
  7.9 0.7 all-gather.8.cloned.1.call-update
  8.6 0.0 all-gather.10.cloned.1.call-start
  8.7 0.7 all-gather.10.cloned.1.call-update
  9.4 0.0 all-gather.12.cloned.1.call-start
  9.4 0.5 all-gather.12.cloned.1.call-update
  10.0 0.0 reduce-scatter.2.cloned.1.call-start
  10.0 0.7 iota_compare_fusion.1
  10.7 0.7 iota_compare_fusion
  11.4 50.6 %all-gather.6.cloned.1.call-done = bf16[768,1024]{0,1:T(8,128)(2,1)} async-done(((bf16[768,64]{0,1:T(8,128)(2,1)}), bf16[768,1024]{0,1:T(8,128)(2,1)}) %all-gather.6.cloned.1.call-update) | async-done | bytes 1572880 | tf_op jit(solution)/shard_map/all_gather | solution.py:50
  62.0 41.4 %all-gather.8.cloned.1.call-done = bf16[1024,1024]{1,0:T(8,128)(2,1)} async-done(((bf16[64,1024]{1,0:T(8,128)(2,1)}), bf16[1024,1024]{1,0:T(8,128)(2,1)}) %all-gather.8.cloned.1.call-update) | async-done | bytes 2097168 | tf_op jit(solution)/shard_map/all_gather | solution.py:17
  103.4 10.5 %fusion.17 = (f32[768]{0:T(1024)S(1)}, f32[768,1024]{1,0:T(8,128)S(1)}) fusion(bf16[768,1024]{0,1:T(8,128)(2,1)} %all-gather.6.cloned.1.call-done, bf16[1024,1024]{1,0:T(8,128)(2,1)} %all-gather.8.cloned.1.call-done), kind=kOutput, calls=%fused_computation.41 | convolution fusion | flops 1661730048 | bytes 6818816 | tf_op jit(solution)/shard_map/dot_general | solution.py:15
  114.0 0.0 copy-start.2
  114.0 0.4 multiply_reduce_fusion
  114.5 82.1 %all-gather.10.cloned.1.call-done = bf16[1024,7936]{1,0:T(8,128)(2,1)} async-done(((bf16[64,7936]{1,0:T(8,128)(2,1)}), bf16[1024,7936]{1,0:T(8,128)(2,1)}) %all-gather.10.cloned.1.call-update) | async-done | bytes 16252944 | tf_op jit(solution)/shard_map/all_gather | solution.py:54
  196.5 0.0 copy-done.2
  196.5 21.4 %convolution_add_fusion = f32[768,7936]{1,0:T(8,128)} fusion(bf16[1024,7936]{1,0:T(8,128)(2,1)} %all-gather.10.cloned.1.call-done, f32[7936]{0:T(1024)S(1)} %copy-done.2, f32[768,1024]{1,0:T(8,128)S(1)} %get-tuple-element.8, f32[768]{0:T(1024)S(1)} %add_rsqrt_fusion, f32[768]{0:T(1024)S(1)} %broadcast_multiply_fusion), kind=kOutput, calls=%fused_computation.1 | convolution fusion | flops 12490702848 | bytes 43815936 | tf_op jit(solution)/shard_map/dot_general | solution.py:52
  217.9 0.0 copy-start.1
  217.9 9.4 %select_reduce_fusion = f32[3,7936]{1,0:T(4,128)S(1)} fusion(f32[3,256,7936]{2,1,0:T(8,128)} %bitcast.14, pred[3,256]{1,0:T(4,128)(4,1)S(1)} %iota_compare_fusion.1), kind=kLoop, calls=%fused_computation | loop fusion | flops 12165888 | bytes 24475392 | tf_op jit(solution)/shard_map/reduce_max | solution.py:29
  227.4 9.2 %all-gather.12.cloned.1.call-done = bf16[128,7936]{1,0:T(8,128)(2,1)} async-done(((bf16[8,7936]{1,0:T(8,128)(2,1)}), bf16[128,7936]{1,0:T(8,128)(2,1)}) %all-gather.12.cloned.1.call-update) | async-done | bytes 2031632 | tf_op jit(solution)/shard_map/all_gather | solution.py:58
  236.5 2.2 convolution_bitcast_fusion
  238.7 34.3 %psum.7 = f32[128,3]{0,1:T(4,128)S(1)} all-reduce(f32[128,3]{0,1:T(4,128)S(1)} %convolution_bitcast_fusion), channel_id=1, replica_groups=mesh['enc'=16,'vocab'=8,'grp'=2] {'vocab','grp'}, use_global_device_ids=true, to_apply=%region_3.4 | all-reduce | flops 384 | bytes 3072 | tf_op jit(solution)/shard_map/psum | solution.py:62
  273.0 15.7 %all-gather = f32[16,3,128]{2,1,0:T(4,128)S(1)} all-gather(f32[1,3,128]{2,1,0:T(4,128)S(1)} %bitcast.17), channel_id=1, replica_groups=mesh['enc'=16,'vocab'=8,'grp'=2] {'enc'}, dimensions={0}, use_global_device_ids=true | all-gather | bytes 26112 | tf_op jit(solution)/shard_map/all_gather | solution.py:63
  288.7 0.0 copy-done.1
  288.8 0.6 subtract_reduce_fusion
  289.4 0.0 copy-start
  289.4 2.7 fusion.14
  292.0 0.0 reduce-scatter.2.cloned.1.call-update
  292.7 0.0 copy-done
  292.7 1.0 fusion.20
  293.8 61.7 %reduce-scatter.2.cloned.1.call-done = f32[8,7936]{1,0:T(8,128)} async-done(((f32[128,7936]{1,0:T(8,128)}), f32[8,7936]{1,0:T(8,128)}) %reduce-scatter.2.cloned.1.call-update) | async-done | bytes 253968 | tf_op jit(solution)/shard_map/reduce_scatter | solution.py:67
  (5 shorter events, 0.1 us)
Async XLA Ops:
  7.2 54.9 %all-gather.6.cloned.1.call-start = ((), (), s32[]{:S(2)}) async-start(), calls=%async_computation.1 | async-start | bytes 1671168 | tf_op jit(solution)/shard_map/all_gather | solution.py:50
  7.9 95.5 %all-gather.8.cloned.1.call-start = ((), (), s32[]{:S(2)}) async-start(), calls=%async_computation.2 | async-start | bytes 2228224 | tf_op jit(solution)/shard_map/all_gather | solution.py:17
  8.6 187.9 %all-gather.10.cloned.1.call-start = ((), (), s32[]{:S(2)}) async-start(), calls=%async_computation.3 | async-start | bytes 17268736 | tf_op jit(solution)/shard_map/all_gather | solution.py:54
  9.4 227.2 %all-gather.12.cloned.1.call-start = ((), (), s32[]{:S(2)}) async-start(), calls=%async_computation.4 | async-start | bytes 2158592 | tf_op jit(solution)/shard_map/all_gather | solution.py:58
  10.0 345.5 %reduce-scatter.2.cloned.1.call-start = ((), (), s32[]{:S(2)}) async-start(), calls=%async_computation.5 | async-start | bytes 4317184 | tf_op jit(solution)/shard_map/reduce_scatter | solution.py:67
  114.0 82.6 %copy-start.2 = (f32[7936]{0:T(1024)S(1)}, f32[7936]{0:T(1024)}, u32[]{:S(2)}) copy-start(f32[7936]{0:T(1024)} %param.10) | copy-start | bytes 95236
  217.9 70.8 %copy-start.1 = (s32[128]{0:T(128)S(1)}, s32[128]{0:T(128)}, u32[]{:S(2)}) copy-start(s32[128]{0:T(128)} %param.13) | copy-start | bytes 1540
  289.4 3.3 copy-start
Sparse Core Ops, SparseCore 0:
  10.5 51.5 all-gather.5
  63.9 39.5 all-gather.7
  105.3 91.2 all-gather.9
  198.2 38.2 all-gather.11
  292.2 63.2 reduce-scatter.1
where the time goes:
time: 363 us
  waiting for transfers between devices  248 us (68%)
  blocking collectives  50 us (14%)
  matrix products  37.8 us (10%)
  between operations  15.6 us (4%)
  other arithmetic  12 us (3%)
    all_gather x1, waiting for transfers between devices, per_device(): lax.all_gather(head_weight, 'enc', axis=0, tiled=True)  82.1 us
    reduce_scatter x1, waiting for transfers between devices, per_device(): lax.psum_scatter(jnp.dot(own_grad, pass_reps, preferred_element_type=jnp....  61.7 us
    all_gather x1, waiting for transfers between devices, per_device(): features_all = lax.all_gather(hidden, ('vocab', 'grp'), axis=1, tiled=True)  50.6 us
    all_gather x1, waiting for transfers between devices, project(): lax.all_gather(dense_weight, 'enc', axis=0, tiled=True)  41.4 us
    psum x1, blocking collectives, per_device(): local_scores = lax.psum(partial_value, ('vocab', 'grp'))  34.3 us
    dot_general x1, matrix products, per_device(): jnp.dot(normed, lax.all_gather(head_weight, 'enc', axis=0, tiled=True), p...  21.4 us
    all_gather x1, blocking collectives, per_device(): scores = lax.all_gather(local_scores, 'enc', axis=1, tiled=True)  15.7 us
    dot_general x1, matrix products, project(): jnp.dot(in_rows, lax.all_gather(dense_weight, 'enc', axis=0, tiled=True),...  10.5 us
  transfers between devices with their start and end apart: 5, of which 5 were waited for; matrix products, arithmetic and copies ran while one was open for 12% of the time, Pallas kernels for 0%

commit v1 on v0

--- a/solution.py
+++ b/solution.py
@@ -59,7 +59,11 @@
     partial_value = lax.dot_general(
         all_queries, pass_reps, (((1,), (1,)), ((), ())), preferred_element_type=jnp.float32
     )
-    local_scores = lax.psum(partial_value, ("vocab", "grp"))
+
+    def do_hubs_up(vec, comm_axis):
+        return jnp.sum(lax.all_gather(vec, comm_axis), 0)
+
+    local_scores = do_hubs_up(partial_value, ("vocab", "grp"))
     scores = lax.all_gather(local_scores, "enc", axis=1, tiled=True)
     loss_sum, score_grad = softmax_grads(scores, positives)
     batch_loss = loss_sum / scores.shape[0]

time: 363 us -> 349 us (0.961)
  blocking collectives: 50 us -> 38.7 us
    psum x1 -> x0, blocking collectives: 34.3 us -> none  [per_device(): local_scores = lax.psum(partial_value, ('vocab', 'grp'))]
    all_gather x0 -> x1, blocking collectives: none -> 23 us  [do_hubs_up(): return jnp.sum(lax.all_gather(vec, comm_axis), 0)]
  transfers between devices with their start and end apart: 5 -> 5, of which waited for: 5 -> 5; matrix products, arithmetic and copies ran while one was open for 12% -> 13% of each run, Pallas kernels for 0% -> 0%
where the time goes in v1:
time: 349 us
  waiting for transfers between devices  245 us (70%)
  blocking collectives  38.7 us (11%)
  matrix products  37.8 us (11%)
  between operations  15.6 us (4%)
  other arithmetic  12 us (3%)
    all_gather x1, waiting for transfers between devices, per_device(): lax.all_gather(head_weight, 'enc', axis=0, tiled=True)  82.1 us
    reduce_scatter x1, waiting for transfers between devices, per_device(): lax.psum_scatter(jnp.dot(own_grad, pass_reps, preferred_element_type=jnp....  59 us
    all_gather x1, waiting for transfers between devices, per_device(): features_all = lax.all_gather(hidden, ('vocab', 'grp'), axis=1, tiled=True)  50.6 us
    all_gather x1, waiting for transfers between devices, project(): lax.all_gather(dense_weight, 'enc', axis=0, tiled=True)  41.4 us
    all_gather x1, blocking collectives, do_hubs_up(): return jnp.sum(lax.all_gather(vec, comm_axis), 0)  23 us
    dot_general x1, matrix products, per_device(): jnp.dot(normed, lax.all_gather(head_weight, 'enc', axis=0, tiled=True), p...  21.4 us
    all_gather x1, blocking collectives, per_device(): scores = lax.all_gather(local_scores, 'enc', axis=1, tiled=True)  15.7 us
    dot_general x1, matrix products, project(): jnp.dot(in_rows, lax.all_gather(dense_weight, 'enc', axis=0, tiled=True),...  10.5 us
  transfers between devices with their start and end apart: 5, of which 5 were waited for; matrix products, arithmetic and copies ran while one was open for 13% of the time, Pallas kernels for 0%

profile of v1, /device:TPU:2, one launch (start us, length us, event | category | flops | bytes accessed | tf_op | source)
XLA Modules:
  0.0 349.2 jit_solution(5108966183055949884)
XLA Ops:
  7.2 0.0 all-gather.7.cloned.1.call-start
  7.2 0.7 all-gather.7.cloned.1.call-update
  7.9 0.0 all-gather.9.cloned.1.call-start
  7.9 0.7 all-gather.9.cloned.1.call-update
  8.6 0.0 all-gather.11.cloned.1.call-start
  8.7 0.7 all-gather.11.cloned.1.call-update
  9.4 0.0 all-gather.13.cloned.1.call-start
  9.4 0.5 all-gather.13.cloned.1.call-update
  10.0 0.0 reduce-scatter.2.cloned.1.call-start
  10.0 0.7 iota_compare_fusion.1
  10.7 0.7 iota_compare_fusion
  11.4 50.6 %all-gather.7.cloned.1.call-done = bf16[768,1024]{0,1:T(8,128)(2,1)} async-done(((bf16[768,64]{0,1:T(8,128)(2,1)}), bf16[768,1024]{0,1:T(8,128)(2,1)}) %all-gather.7.cloned.1.call-update) | async-done | bytes 1572880 | tf_op jit(solution)/shard_map/all_gather | solution.py:50
  62.0 41.4 %all-gather.9.cloned.1.call-done = bf16[1024,1024]{1,0:T(8,128)(2,1)} async-done(((bf16[64,1024]{1,0:T(8,128)(2,1)}), bf16[1024,1024]{1,0:T(8,128)(2,1)}) %all-gather.9.cloned.1.call-update) | async-done | bytes 2097168 | tf_op jit(solution)/shard_map/all_gather | solution.py:17
  103.4 10.5 %fusion.17 = (f32[768]{0:T(1024)S(1)}, f32[768,1024]{1,0:T(8,128)S(1)}) fusion(bf16[768,1024]{0,1:T(8,128)(2,1)} %all-gather.7.cloned.1.call-done, bf16[1024,1024]{1,0:T(8,128)(2,1)} %all-gather.9.cloned.1.call-done), kind=kOutput, calls=%fused_computation.42 | convolution fusion | flops 1661730048 | bytes 6818816 | tf_op jit(solution)/shard_map/dot_general | solution.py:15
  114.0 0.0 copy-start.2
  114.0 0.4 multiply_reduce_fusion
  114.5 82.1 %all-gather.11.cloned.1.call-done = bf16[1024,7936]{1,0:T(8,128)(2,1)} async-done(((bf16[64,7936]{1,0:T(8,128)(2,1)}), bf16[1024,7936]{1,0:T(8,128)(2,1)}) %all-gather.11.cloned.1.call-update) | async-done | bytes 16252944 | tf_op jit(solution)/shard_map/all_gather | solution.py:54
  196.5 0.0 copy-done.2
  196.5 21.4 %convolution_add_fusion = f32[768,7936]{1,0:T(8,128)} fusion(bf16[1024,7936]{1,0:T(8,128)(2,1)} %all-gather.11.cloned.1.call-done, f32[7936]{0:T(1024)S(1)} %copy-done.2, f32[768,1024]{1,0:T(8,128)S(1)} %get-tuple-element.8, f32[768]{0:T(1024)S(1)} %add_rsqrt_fusion, f32[768]{0:T(1024)S(1)} %broadcast_multiply_fusion), kind=kOutput, calls=%fused_computation.1 | convolution fusion | flops 12490702848 | bytes 43815936 | tf_op jit(solution)/shard_map/dot_general | solution.py:52
  217.9 0.0 copy-start.1
  217.9 9.4 %select_reduce_fusion = f32[3,7936]{1,0:T(4,128)S(1)} fusion(f32[3,256,7936]{2,1,0:T(8,128)} %bitcast.19, pred[3,256]{1,0:T(4,128)(4,1)S(1)} %iota_compare_fusion.1), kind=kLoop, calls=%fused_computation | loop fusion | flops 12165888 | bytes 24475392 | tf_op jit(solution)/shard_map/reduce_max | solution.py:29
  227.4 9.2 %all-gather.13.cloned.1.call-done = bf16[128,7936]{1,0:T(8,128)(2,1)} async-done(((bf16[8,7936]{1,0:T(8,128)(2,1)}), bf16[128,7936]{1,0:T(8,128)(2,1)}) %all-gather.13.cloned.1.call-update) | async-done | bytes 2031632 | tf_op jit(solution)/shard_map/all_gather | solution.py:58
  236.5 2.2 convolution_bitcast_fusion
  238.7 23.0 %all-gather = f32[2048,3]{0,1:T(4,128)S(1)} all-gather(f32[128,3]{0,1:T(4,128)S(1)} %convolution_bitcast_fusion), channel_id=2, replica_groups=mesh['enc'=16,'vocab'=8,'grp'=2] {'vocab','grp'}, dimensions={0}, use_global_device_ids=true | all-gather | bytes 26112 | tf_op jit(solution)/shard_map/all_gather | solution.py:64
  261.8 15.7 %all-gather.1 = f32[16,3,128]{2,1,0:T(4,128)S(1)} all-gather(f32[1,3,128]{2,1,0:T(4,128)S(1)} %bitcast.23), channel_id=1, replica_groups=mesh['enc'=16,'vocab'=8,'grp'=2] {'enc'}, dimensions={0}, use_global_device_ids=true | all-gather | bytes 26112 | tf_op jit(solution)/shard_map/all_gather | solution.py:67
  277.5 0.0 copy-done.1
  277.5 0.6 subtract_reduce_fusion
  278.1 0.0 copy-start
  278.1 2.7 fusion.14
  280.8 0.0 reduce-scatter.2.cloned.1.call-update
  281.5 0.0 copy-done
  281.5 1.0 fusion.20
  282.5 59.0 %reduce-scatter.2.cloned.1.call-done = f32[8,7936]{1,0:T(8,128)} async-done(((f32[128,7936]{1,0:T(8,128)}), f32[8,7936]{1,0:T(8,128)}) %reduce-scatter.2.cloned.1.call-update) | async-done | bytes 253968 | tf_op jit(solution)/shard_map/reduce_scatter | solution.py:71
  (6 shorter events, 0.1 us)
Async XLA Ops:
  7.2 54.9 %all-gather.7.cloned.1.call-start = ((), (), s32[]{:S(2)}) async-start(), calls=%async_computation.1 | async-start | bytes 1671168 | tf_op jit(solution)/shard_map/all_gather | solution.py:50
  7.9 95.5 %all-gather.9.cloned.1.call-start = ((), (), s32[]{:S(2)}) async-start(), calls=%async_computation.2 | async-start | bytes 2228224 | tf_op jit(solution)/shard_map/all_gather | solution.py:17
  8.6 187.9 %all-gather.11.cloned.1.call-start = ((), (), s32[]{:S(2)}) async-start(), calls=%async_computation.3 | async-start | bytes 17268736 | tf_op jit(solution)/shard_map/all_gather | solution.py:54
  9.4 227.2 %all-gather.13.cloned.1.call-start = ((), (), s32[]{:S(2)}) async-start(), calls=%async_computation.4 | async-start | bytes 2158592 | tf_op jit(solution)/shard_map/all_gather | solution.py:58
  10.0 331.6 %reduce-scatter.2.cloned.1.call-start = ((), (), s32[]{:S(2)}) async-start(), calls=%async_computation.5 | async-start | bytes 4317184 | tf_op jit(solution)/shard_map/reduce_scatter | solution.py:71
  114.0 82.6 %copy-start.2 = (f32[7936]{0:T(1024)S(1)}, f32[7936]{0:T(1024)}, u32[]{:S(2)}) copy-start(f32[7936]{0:T(1024)} %param.10) | copy-start | bytes 95236
  217.9 59.6 %copy-start.1 = (s32[128]{0:T(128)S(1)}, s32[128]{0:T(128)}, u32[]{:S(2)}) copy-start(s32[128]{0:T(128)} %param.13) | copy-start | bytes 1540
  278.1 3.3 copy-start
Sparse Core Ops, SparseCore 0:
  10.5 51.5 all-gather.6
  63.9 39.5 all-gather.8
  105.3 91.2 all-gather.10
  198.2 38.2 all-gather.12
  280.9 60.5 reduce-scatter.1
